TPU v7x, 32 devices: a whole 2x2x4 slice. The times are simulated.
32 devices in a mesh: seq: 8 (over z, x), tp: 4 (over y, core).
Axes of the slice: x: 2, y: 2, z: 4, core: 2. Of those that a mesh axis runs over, the one named last changes fastest.
Arguments:
- hidden_new: bfloat16 [3, 16, 8192], P(None, None, 'seq'), may hold values from -6 to 6
- w_kv: bfloat16 [8192, 8, 256], P('seq', 'tp'), may hold values from -0.0625 to 0.0625
- w_out: bfloat16 [8192, 8192], P('tp', 'seq'), may hold values from -0.0625 to 0.0625
- queries_draft: bfloat16 [3, 4, 8, 32, 128], P(None, None, 'tp'), may hold values from -48 to 48
- queries_verify: bfloat16 [3, 4, 8, 32, 128], P(None, None, 'tp'), may hold values from -48 to 48
- keys_cache: bfloat16 [4, 8, 16384, 128], P(None, 'tp', 'seq'), may hold values from -6 to 6
- values_cache: bfloat16 [4, 8, 16384, 128], P(None, 'tp', 'seq'), may hold values from -6 to 6
- key_levels: bfloat16 [4, 8, 16384, 128], P(None, 'tp', 'seq'), may hold values from -8 to 7, as said below
- value_levels: bfloat16 [4, 8, 16384, 128], P(None, 'tp', 'seq'), may hold values from -8 to 7, as said below
- key_scales: float32 [4, 8, 16384], P(None, 'tp', 'seq'), may hold values from 0.05 to 0.5
- value_scales: float32 [4, 8, 16384], P(None, 'tp', 'seq'), may hold values from 0.1 to 0.4
- lengths: int32 [4], replicated, may hold values from 2 to 16376, as said below
- accepted: int32 [2, 4], replicated, may hold values from 0 to 4, as said below
Outputs:
- layer_out: bfloat16 [3, 2, 16, 8192], P(None, None, None, 'seq')
Inputs may be any that keep to these rules, and one draw needn't show every extreme that they name: `key_levels`: every entry is a whole number. Positions 0 and 1 of every sequence and head hold equal levels. `value_levels`: every entry is a whole number. `lengths`: some sequence starts with exactly 16376 valid positions, another with 16 or fewer. `accepted`: the values 0 and 4 both occur.
All inputs are finite; a program needn't handle non-finite values.
Results may differ from a plain program's by a relative error of at most 0.006.
The roundings to bfloat16 on the way count: a program that leaves them out, or rounds other values in their place, can miss the bound.
Values may be sent and summed in bfloat16 or wider, within the bound.
A program may use at most 128 MiB of HBM per device.

v0:
```python
import math

import jax
import jax.numpy as jnp
from jax import lax
from jax.sharding import PartitionSpec as P

HD = 128
GROUP = 8
R = 4
ROUNDS = 3


NEG = -1e30


def dequantize(levels, scales):
    return (levels.astype(jnp.float32) * scales[..., None]).astype(jnp.bfloat16)


def attend(queries, keys, values, usable):
    scores = jnp.einsum("bhqd,bhkd->bhqk", queries, keys, preferred_element_type=jnp.float32) * (
        1.0 / math.sqrt(HD)
    )
    scores = jnp.where(usable, scores, NEG)
    maxima = jnp.max(scores, axis=-1)
    weights = jnp.where(usable, jnp.exp(scores - maxima[..., None]), 0.0).astype(jnp.bfloat16)
    totals = jnp.sum(weights.astype(jnp.float32), axis=-1)
    weighted = jnp.einsum("bhqk,bhkd->bhqd", weights, values, preferred_element_type=jnp.float32)
    return (maxima, totals, weighted)


def combine(former, latter):
    highest = jnp.maximum(former[0], latter[0])
    former_w = jnp.exp(former[0] - highest)
    latter_w = jnp.exp(latter[0] - highest)
    return (
        highest,
        former[1] * former_w + latter[1] * latter_w,
        former[2] * former_w[..., None] + latter[2] * latter_w[..., None],
    )


def finish(partial_value):
    return (partial_value[2] / partial_value[1][..., None]).astype(jnp.bfloat16)


def arrange(attended):
    kind_count, batch_size, head_count, query_rows, head_width = attended.shape
    split_rows = attended.reshape(kind_count, batch_size, head_count, GROUP, R, head_width)
    return split_rows.transpose(0, 1, 4, 2, 3, 5).reshape(
        kind_count * batch_size * R, head_count * GROUP * head_width
    )


def stacked_rows(draft_part, verify_part):
    maxima = jnp.stack([draft_part[0], verify_part[0]]).reshape(1, -1)
    totals = jnp.stack([draft_part[1], verify_part[1]]).reshape(1, -1)
    weighted = jnp.stack([draft_part[2], verify_part[2]]).reshape(1, maxima.shape[1], -1)
    return (maxima, totals, weighted)


def spread_merge(draft_part, verify_part, draft_self, verify_self, seq_index):
    maxima, totals, weighted = stacked_rows(draft_part, verify_part)
    maxima, totals, weighted = (
        lax.all_to_all(maxima, "seq", split_axis=1, concat_axis=0, tiled=True),
        lax.all_to_all(totals, "seq", split_axis=1, concat_axis=0, tiled=True),
        lax.all_to_all(weighted, "seq", split_axis=1, concat_axis=0, tiled=True),
    )
    highest = jnp.max(maxima, axis=0)
    factors = jnp.exp(maxima - highest[None])
    share_part = (
        highest,
        jnp.sum(totals * factors, axis=0),
        jnp.sum(weighted * factors[..., None], axis=0),
    )
    share_rows = highest.shape[0]
    self_max, self_tot, self_sum = stacked_rows(draft_self, verify_self)
    row_start = seq_index * share_rows
    self_share = (
        lax.dynamic_slice_in_dim(self_max[0], row_start, share_rows, 0),
        lax.dynamic_slice_in_dim(self_tot[0], row_start, share_rows, 0),
        lax.dynamic_slice_in_dim(self_sum[0], row_start, share_rows, 0),
    )
    merged = finish(combine(share_part, self_share))
    gathered = lax.all_gather(merged, "seq", axis=0, tiled=True)
    return gathered.reshape((2,) + draft_part[2].shape)


def per_device(
    hidden_new,
    w_kv,
    w_out,
    queries_draft,
    queries_verify,
    keys_cache,
    values_cache,
    key_levels,
    value_levels,
    key_scales,
    value_scales,
    lengths,
    accepted,
):
    batch_size, head_count, local_len, head_width = keys_cache.shape
    seq_index = lax.axis_index("seq")
    first_row = seq_index * local_len
    key_low = dequantize(key_levels, key_scales)
    value_low = dequantize(value_levels, value_scales)
    places = first_row + jnp.arange(local_len, dtype=jnp.int32)
    stored = (places[None, :] < lengths[:, None])[:, None, :, None]
    flat_kv = w_kv.reshape(w_kv.shape[0], -1)
    tokens = jnp.arange(GROUP * R, dtype=jnp.int32) % R
    causal = (tokens[:, None] >= jnp.arange(R, dtype=jnp.int32)[None, :])[None, None]
    offsets = jnp.arange(R, dtype=jnp.int32)[None, :]
    batch_rows = jnp.broadcast_to(jnp.arange(batch_size, dtype=jnp.int32)[:, None], (batch_size, R))
    length_now = lengths
    results = []
    for turn_index in range(ROUNDS):
        partial_kv = jnp.dot(hidden_new[turn_index], flat_kv, preferred_element_type=jnp.float32)
        fresh_rows = (
            lax.psum(partial_kv, "seq")
            .astype(jnp.bfloat16)
            .reshape(batch_size, R, head_count, 2, head_width)
        )
        new_keys = fresh_rows[:, :, :, 0].transpose(0, 2, 1, 3)
        new_values = fresh_rows[:, :, :, 1].transpose(0, 2, 1, 3)
        usable = (places[None, :] < length_now[:, None])[:, None, None, :]
        draft_q = queries_draft[turn_index]
        verify_q = queries_verify[turn_index]
        draft_keys = jnp.where(stored, key_low, keys_cache)
        draft_values = jnp.where(stored, value_low, values_cache)
        draft_part = attend(draft_q, draft_keys, draft_values, usable)
        draft_self = attend(draft_q, new_keys, new_values, causal)
        verify_part = attend(verify_q, keys_cache, values_cache, usable)
        verify_self = attend(verify_q, new_keys, new_values, causal)
        attended = spread_merge(draft_part, verify_part, draft_self, verify_self, seq_index)
        projected = jnp.dot(arrange(attended), w_out, preferred_element_type=jnp.float32)
        summed = lax.psum(projected, "tp")
        results.append(summed.astype(jnp.bfloat16).reshape(2, batch_size * R, -1))
        if turn_index + 1 < ROUNDS:
            accepted_now = accepted[turn_index]
            targets = length_now[:, None] + offsets - first_row
            landing = (offsets < accepted_now[:, None]) & (targets >= 0) & (targets < local_len)
            targets = jnp.where(landing, targets, local_len)
            keys_cache = keys_cache.at[batch_rows, :, targets, :].set(
                fresh_rows[:, :, :, 0], mode="drop"
            )
            values_cache = values_cache.at[batch_rows, :, targets, :].set(
                fresh_rows[:, :, :, 1], mode="drop"
            )
            length_now = length_now + accepted_now
    return jnp.stack(results)


def solution(mesh):
    return jax.shard_map(
        per_device,
        mesh=mesh,
        in_specs=(
            P(None, None, "seq"),
            P("seq", "tp", None),
            P("tp", "seq"),
            P(None, None, "tp", None, None),
            P(None, None, "tp", None, None),
            P(None, "tp", "seq", None),
            P(None, "tp", "seq", None),
            P(None, "tp", "seq", None),
            P(None, "tp", "seq", None),
            P(None, "tp", "seq"),
            P(None, "tp", "seq"),
            P(),
            P(),
        ),
        out_specs=P(None, None, None, "seq"),
        check_vma=False,
    )
```

profile of v0, /device:TPU:0, one launch (start us, length us, event | category | flops | bytes accessed | tf_op | source)
XLA Modules:
  0.0 336.0 jit_solution(9079900889281217494)
XLA Ops:
  0.0 4.6 %copy.174 = bf16[4,2,2048,128]{3,2,1,0:T(8,128)(2,1)} copy(bf16[4,2,2048,128]{3,2,1,0:T(8,128)(2,1)} %param.18) | data formatting | bytes 8388608
  4.6 2.0 copy.175
  6.7 3.9 %fusion.169 = (f32[4,2,32]{2,1,0:T(2,128)S(1)}, f32[4,2,32,2048]{3,2,1,0:T(8,128)S(1)}) fusion(bf16[4,2,2048,128]{3,2,1,0:T(8,128)(2,1)} %copy.174, bf16[3,4,2,32,128]{4,3,2,1,0:T(8,128)(2,1)S(1)} %copy-done.16, pred[4,2048]{1,0:T(4,128)(4,1)S(1)} %get-tuple-element.48), kind=kOutput, calls=%fused_computation.242 | convolution fusion | flops 135790336 | bytes 6366208 | tf_op jit(solution)/shard_map/bhqd,bhkd->bhqk/dot_general | solution.py:22
  10.7 5.9 %fusion.170 = (f32[4,2,32]{2,1,0:T(2,128)S(1)}, f32[4,2,32,2048]{3,2,1,0:T(8,128)S(1)}) fusion(bf16[3,4,2,32,128]{4,3,2,1,0:T(8,128)(2,1)} %param.16, bf16[4,2,2048,128]{3,2,1,0:T(8,128)(2,1)S(1)} %copy-done.2, pred[4,2048]{1,0:T(4,128)(4,1)S(1)} %get-tuple-element.48, f32[4,2,2048]{2,1,0:T(2,128)S(1)} %copy-done.22, bf16[4,2,2048,128]{3,2,1,0:T(8,128)(2,1)} %param.20), kind=kOutput, calls=%fused_computation.243 | convolution fusion | flops 144178944 | bytes 10634240 | tf_op jit(solution)/shard_map/bhqd,bhkd->bhqk/dot_general | solution.py:22
  16.6 0.9 convert_reduce_fusion.5
  17.5 0.4 copy-done.8
  17.9 0.7 all_to_all.104
  18.6 7.3 %all-to-all-start.2 = ((f32[1,8,64]{2,0,1:T(1,128)}), f32[1,8,64]{2,0,1:T(1,128)S(1)}, u32[]{:S(2)}, u32[]{:S(2)}) async-start(f32[1,8,64]{2,0,1:T(1,128)} %all_to_all.104), calls=%async_computation.2 | async-start | bytes 8192 | tf_op jit(solution)/shard_map/all_to_all | solution.py:67
  25.9 0.2 copy.99
  26.1 0.2 fusion.111
  26.4 0.3 fusion.113
  26.6 0.3 fusion.115
  26.9 38.5 %all-reduce = (bf16[16,512]{1,0:T(8,128)(2,1)S(1)}, bf16[16,512]{1,0:T(8,128)(2,1)S(1)}, bf16[16,512]{1,0:T(8,128)(2,1)S(1)}) all-reduce(f32[16,512]{1,0:T(8,128)S(1)} %fusion.111, f32[16,512]{1,0:T(8,128)S(1)} %fusion.115, f32[16,512]{1,0:T(8,128)S(1)} %fusion.113), channel_id=1, replica_groups=mesh['seq'=8,'tp'=4] {'seq'}, use_global_device_ids=true, to_apply=%region_34.35 | all-reduce | flops 24576 | bytes 147456 | tf_op jit(solution)/shard_map/psum | solution.py:122
  66.8 2.6 scatter_fusion
  69.4 10.5 %copy.76 = bf16[4,2,2048,128]{3,1,2,0:T(2,128)(2,1)} copy(bf16[4,2,2048,128]{3,2,1,0:T(8,128)(2,1)} %scatter_fusion) | data formatting | bytes 8388608 | tf_op jit(solution)/shard_map/scatter | solution.py:146
  80.0 2.6 scatter_fusion.2
  82.6 8.5 %fusion.162 = (f32[4,2,32]{2,1,0:T(2,128)S(1)}, f32[4,2,32,2048]{3,2,1,0:T(8,128)}) fusion(bf16[3,4,2,32,128]{4,3,2,1,0:T(8,128)(2,1)S(1)} %copy-done.21, pred[4,2048]{1,0:T(4,128)(4,1)S(1)} %get-tuple-element.48, bf16[4,2,2048,128]{3,1,2,0:T(2,128)(2,1)} %scatter_fusion.2, f32[4,2,2048]{2,1,0:T(2,128)S(1)} %copy-done.23, ...), kind=kOutput, calls=%fused_computation.235 | convolution fusion | flops 144178944 | bytes 10634240 | tf_op jit(solution)/shard_map/bhqd,bhkd->bhqk/dot_general | solution.py:22
  91.1 2.9 fusion.161
  94.0 6.2 %fusion.168 = (f32[4,2,32]{2,1,0:T(2,128)S(1)}, f32[4,2,32,2048]{3,2,1,0:T(8,128)}) fusion(bf16[3,4,2,32,128]{4,3,2,1,0:T(8,128)(2,1)S(1)} %copy-done.21, bf16[4,2,2048,128]{3,2,1,0:T(8,128)(2,1)S(1)} %copy-done.3, pred[4,2048]{1,0:T(4,128)(4,1)S(1)} %get-tuple-element.48, f32[4,2,2048]{2,1,0:T(2,128)S(1)} %copy-done.23, ...), kind=kOutput, calls=%fused_computation.241 | convolution fusion | flops 144178944 | bytes 10634240 | tf_op jit(solution)/shard_map/bhqd,bhkd->bhqk/dot_general | solution.py:22
  100.2 2.8 fusion.167
  103.1 0.9 convolution_bitcast_fusion.1
  104.0 0.6 copy-done.9
  104.7 1.2 copy-done.20
  105.9 4.2 %fusion.66 = f32[1,4,2,32,128]{4,3,2,1,0:T(8,128)S(1)} fusion(bf16[4,2,2048,128]{3,2,1,0:T(8,128)(2,1)S(1)} %copy-done, pred[4,2048]{1,0:T(4,128)(4,1)S(1)} %get-tuple-element.48, f32[4,2,2048]{2,1,0:T(2,128)S(1)} %copy-done.24, bf16[4,2,2048,128]{3,2,1,0:T(8,128)(2,1)S(1)} %copy-done.20, f32[4,2,32,2048]{3,2,1,0:T(8,128)S(1)} %copy-done.9, ...), kind=kOutput, calls=%fused_computation.62 | convolution fusion | flops 144179200 | bytes 10691584 | tf_op jit(solution)/shard_map/bhqk,bhkd->bhqd/dot_general | solution.py:29
  110.2 0.7 pad_maximum_fusion
  110.9 2.6 scatter_fusion.1
  113.4 10.6 %copy.80 = bf16[4,2,2048,128]{3,1,2,0:T(2,128)(2,1)} copy(bf16[4,2,2048,128]{3,2,1,0:T(8,128)(2,1)} %scatter_fusion.1) | data formatting | bytes 8388608 | tf_op jit(solution)/shard_map/scatter | solution.py:149
  124.1 6.0 %fusion.69 = f32[1,4,2,32,128]{4,3,2,1,0:T(8,128)S(1)} fusion(bf16[4,2,2048,128]{3,2,1,0:T(8,128)(2,1)S(1)} %copy-done.1, pred[4,2048]{1,0:T(4,128)(4,1)S(1)} %get-tuple-element.48, f32[4,2,2048]{2,1,0:T(2,128)S(1)} %copy-done.24, bf16[4,2,2048,128]{3,2,1,0:T(8,128)(2,1)} %param.21, f32[4,2,32,2048]{3,2,1,0:T(8,128)S(1)} %copy-done.12, ...), kind=kOutput, calls=%fused_computation.63 | convolution fusion | flops 144179200 | bytes 10699776 | tf_op jit(solution)/shard_map/bhqk,bhkd->bhqd/dot_general | solution.py:29
  130.1 0.9 convolution_bitcast_fusion
  131.0 2.6 scatter_fusion.3
  133.6 7.2 %fusion.72 = f32[1,4,2,32,128]{4,3,2,1,0:T(8,128)S(1)} fusion(pred[4,2048]{1,0:T(4,128)(4,1)S(1)} %get-tuple-element.48, bf16[4,2,2048,128]{3,1,2,0:T(2,128)(2,1)} %scatter_fusion.3, f32[4,2,2048]{2,1,0:T(2,128)S(1)} %copy-done.24, bf16[4,2,2048,128]{3,2,1,0:T(8,128)(2,1)} %param.21, f32[4,2,32,2048]{3,2,1,0:T(8,128)} %get-tuple-element.58, ...), kind=kOutput, calls=%fused_computation.64 | convolution fusion | flops 144179200 | bytes 10699776 | tf_op jit(solution)/shard_map/bhqk,bhkd->bhqd/dot_general | solution.py:29
  140.9 1.9 convert_reduce_fusion.1
  142.8 0.3 copy-done.5
  143.1 1.0 fusion.63
  144.3 0.2 convolution_bitcast_fusion.7
  145.7 0.7 pad_maximum_fusion.2
  146.4 0.7 pad_maximum_fusion.4
  147.2 0.7 all_to_all.101
  147.9 3.2 all-to-all-start.1
  151.1 0.7 all_to_all.109
  151.8 5.7 %all-to-all-done.1 = f32[1,8,64]{2,0,1:T(1,128)S(1)} async-done(((f32[1,8,64]{2,0,1:T(1,128)}), f32[1,8,64]{2,0,1:T(1,128)S(1)}, u32[]{:S(2)}, u32[]{:S(2)}) %all-to-all-start.1) | async-done | bytes 2080 | tf_op jit(solution)/shard_map/all_to_all | solution.py:66
  157.5 3.3 all-to-all-start.4
  161.0 0.7 all_to_all.112
  161.9 0.7 all_to_all.120
  162.6 0.7 all_to_all.117
  163.4 3.8 %all-to-all-done.4 = f32[1,8,64]{2,0,1:T(1,128)S(1)} async-done(((f32[1,8,64]{2,0,1:T(1,128)}), f32[1,8,64]{2,0,1:T(1,128)S(1)}, u32[]{:S(2)}, u32[]{:S(2)}) %all-to-all-start.4) | async-done | bytes 2080 | tf_op jit(solution)/shard_map/all_to_all | solution.py:66
  167.3 3.3 all-to-all-start.5
  170.6 6.4 %all-to-all-done.5 = f32[1,8,64]{2,0,1:T(1,128)S(1)} async-done(((f32[1,8,64]{2,0,1:T(1,128)}), f32[1,8,64]{2,0,1:T(1,128)S(1)}, u32[]{:S(2)}, u32[]{:S(2)}) %all-to-all-start.5) | async-done | bytes 2080 | tf_op jit(solution)/shard_map/all_to_all | solution.py:67
  177.0 3.3 all-to-all-start.8
  180.3 6.3 %all-to-all-done.8 = f32[1,8,64]{2,0,1:T(1,128)S(1)} async-done(((f32[1,8,64]{2,0,1:T(1,128)}), f32[1,8,64]{2,0,1:T(1,128)S(1)}, u32[]{:S(2)}, u32[]{:S(2)}) %all-to-all-start.8) | async-done | bytes 2080 | tf_op jit(solution)/shard_map/all_to_all | solution.py:67
  186.7 3.2 all-to-all-start.7
  190.0 6.3 %all-to-all-done.7 = f32[1,8,64]{2,0,1:T(1,128)S(1)} async-done(((f32[1,8,64]{2,0,1:T(1,128)}), f32[1,8,64]{2,0,1:T(1,128)S(1)}, u32[]{:S(2)}, u32[]{:S(2)}) %all-to-all-start.7) | async-done | bytes 2080 | tf_op jit(solution)/shard_map/all_to_all | solution.py:66
  196.3 3.4 %all-to-all-start = ((f32[1,512,128]{2,0,1:T(1,128)}), f32[1,512,128]{2,0,1:T(1,128)S(1)}, u32[]{:S(2)}, u32[]{:S(2)}) async-start(f32[1,512,128]{2,0,1:T(1,128)} %bitcast.6), calls=%async_computation | async-start | bytes 524288 | tf_op jit(solution)/shard_map/all_to_all | solution.py:68
  200.0 7.9 %all-to-all-done = f32[1,512,128]{2,0,1:T(1,128)S(1)} async-done(((f32[1,512,128]{2,0,1:T(1,128)}), f32[1,512,128]{2,0,1:T(1,128)S(1)}, u32[]{:S(2)}, u32[]{:S(2)}) %all-to-all-start) | async-done | bytes 262176 | tf_op jit(solution)/shard_map/all_to_all | solution.py:68
  207.9 3.4 %all-to-all-start.3 = ((f32[1,512,128]{2,0,1:T(1,128)}), f32[1,512,128]{2,0,1:T(1,128)S(1)}, u32[]{:S(2)}, u32[]{:S(2)}) async-start(f32[1,512,128]{2,0,1:T(1,128)} %bitcast.43), calls=%async_computation.3 | async-start | bytes 524288 | tf_op jit(solution)/shard_map/all_to_all | solution.py:68
  211.6 32.1 %all_gather.9 = bf16[512,128]{1,0:T(8,128)(2,1)S(1)} all-gather(bf16[64,128]{1,0:T(8,128)(2,1)S(1)} %divide_convert_fusion.2), channel_id=1, replica_groups=mesh['seq'=8,'tp'=4] {'seq'}, dimensions={0}, use_global_device_ids=true | all-gather | bytes 147456 | tf_op jit(solution)/shard_map/all_gather | solution.py:86
  243.7 3.0 fusion.171
  246.8 4.5 %all-to-all-start.6 = ((f32[1,512,128]{2,0,1:T(1,128)}), f32[1,512,128]{2,0,1:T(1,128)S(1)}, u32[]{:S(2)}, u32[]{:S(2)}) async-start(f32[1,512,128]{2,0,1:T(1,128)} %bitcast.80), calls=%async_computation.6 | async-start | bytes 524288 | tf_op jit(solution)/shard_map/all_to_all | solution.py:68
  251.5 32.0 %all_gather.10 = bf16[512,128]{1,0:T(8,128)(2,1)S(1)} all-gather(bf16[64,128]{1,0:T(8,128)(2,1)S(1)} %divide_convert_fusion.1), channel_id=1, replica_groups=mesh['seq'=8,'tp'=4] {'seq'}, dimensions={0}, use_global_device_ids=true | all-gather | bytes 147456 | tf_op jit(solution)/shard_map/all_gather | solution.py:86
  283.6 3.0 fusion.172
  286.8 30.5 %all_gather.11 = bf16[512,128]{1,0:T(8,128)(2,1)S(1)} all-gather(bf16[64,128]{1,0:T(8,128)(2,1)S(1)} %divide_convert_fusion), channel_id=1, replica_groups=mesh['seq'=8,'tp'=4] {'seq'}, dimensions={0}, use_global_device_ids=true | all-gather | bytes 147456 | tf_op jit(solution)/shard_map/all_gather | solution.py:86
  317.5 3.0 fusion.173
  320.5 14.8 %all-reduce.3 = (bf16[32,1024]{1,0:T(8,128)(2,1)S(1)}, bf16[32,1024]{1,0:T(8,128)(2,1)S(1)}, bf16[32,1024]{1,0:T(8,128)(2,1)S(1)}) all-reduce(f32[32,1024]{1,0:T(8,128)S(1)} %fusion.173, f32[32,1024]{1,0:T(8,128)S(1)} %fusion.172, f32[32,1024]{1,0:T(8,128)S(1)} %fusion.171), channel_id=1, replica_groups=mesh['seq'=8,'tp'=4] {'tp'}, use_global_device_ids=true, to_apply=%region_42.43 | all-reduce | flops 98304 | bytes 589824 | tf_op jit(solution)/shard_map/psum | solution.py:139
  335.3 0.7 pad_maximum_fusion.6
  (125 shorter events, 4.9 us)
Async XLA Ops:
  0.0 4.6 %copy-start.7 = (bf16[4,2,2048,128]{3,2,1,0:T(8,128)(2,1)S(1)}, bf16[4,2,2048,128]{3,2,1,0:T(8,128)(2,1)}, u32[]{:S(2)}) copy-start(bf16[4,2,2048,128]{3,2,1,0:T(8,128)(2,1)} %param.19) | copy-start | bytes 12582916
  4.6 2.0 copy-start.17
  4.6 2.0 copy-start.18
  4.6 2.1 copy-start.16
  6.7 4.0 %copy-start.2 = (bf16[4,2,2048,128]{3,2,1,0:T(8,128)(2,1)S(1)}, bf16[4,2,2048,128]{3,2,1,0:T(8,128)(2,1)}, u32[]{:S(2)}) copy-start(bf16[4,2,2048,128]{3,2,1,0:T(8,128)(2,1)} %copy.174) | copy-start | bytes 12582916
  6.7 4.0 %copy-start.22 = (f32[4,2,2048]{2,1,0:T(2,128)S(1)}, f32[4,2,2048]{2,1,0:T(2,128)}, u32[]{:S(2)}) copy-start(f32[4,2,2048]{2,1,0:T(2,128)} %param.22) | copy-start | bytes 196612
  16.6 1.3 copy-start.8
  16.6 9.3 %copy-start.14 = (bf16[1024,2,256]{2,1,0:T(2,128)(2,1)S(1)}, bf16[1024,2,256]{2,1,0:T(2,128)(2,1)}, u32[]{:S(2)}) copy-start(bf16[1024,2,256]{2,1,0:T(2,128)(2,1)} %param.14) | copy-start | bytes 3145732
  17.9 8.2 %copy-start.15 = (bf16[3,16,1024]{2,1,0:T(8,128)(2,1)S(1)}, bf16[3,16,1024]{2,1,0:T(8,128)(2,1)}, u32[]{:S(2)}) copy-start(bf16[3,16,1024]{2,1,0:T(8,128)(2,1)} %param.13) | copy-start | bytes 294916
  18.6 129.3 %all-to-all-start.2 = ((f32[1,8,64]{2,0,1:T(1,128)}), f32[1,8,64]{2,0,1:T(1,128)S(1)}, u32[]{:S(2)}, u32[]{:S(2)}) async-start(f32[1,8,64]{2,0,1:T(1,128)} %all_to_all.104), calls=%async_computation.2 | async-start | bytes 8192 | tf_op jit(solution)/shard_map/all_to_all | solution.py:67
  26.1 39.5 %copy-start.21 = (bf16[3,4,2,32,128]{4,3,2,1,0:T(8,128)(2,1)S(1)}, bf16[3,4,2,32,128]{4,3,2,1,0:T(8,128)(2,1)}, u32[]{:S(2)}) copy-start(bf16[3,4,2,32,128]{4,3,2,1,0:T(8,128)(2,1)} %param.16) | copy-start | bytes 589828
  69.4 13.2 %copy-start.23 = (f32[4,2,2048]{2,1,0:T(2,128)S(1)}, f32[4,2,2048]{2,1,0:T(2,128)}, u32[]{:S(2)}) copy-start(f32[4,2,2048]{2,1,0:T(2,128)} %param.22) | copy-start | bytes 196612
  82.6 8.5 %copy-start.6 = (bf16[4,2,2048,128]{3,1,2,0:T(2,128)(2,1)S(1)}, bf16[4,2,2048,128]{3,1,2,0:T(2,128)(2,1)}, u32[]{:S(2)}) copy-start(bf16[4,2,2048,128]{3,1,2,0:T(2,128)(2,1)} %scatter_fusion.2) | copy-start | bytes 12582916
  82.6 11.4 %copy-start.19 = (bf16[4,2,2048,128]{3,2,1,0:T(8,128)(2,1)S(1)}, bf16[4,2,2048,128]{3,2,1,0:T(8,128)(2,1)}, u32[]{:S(2)}) copy-start(bf16[4,2,2048,128]{3,2,1,0:T(8,128)(2,1)} %param.20) | copy-start | bytes 12582916
  91.1 2.9 copy-start.3
  100.2 2.8 copy-start
  103.1 1.6 copy-start.9
  103.1 2.8 copy-start.20
  103.1 2.8 copy-start.24
  113.4 10.6 %copy-start.1 = (bf16[4,2,2048,128]{3,2,1,0:T(8,128)(2,1)S(1)}, bf16[4,2,2048,128]{3,2,1,0:T(8,128)(2,1)}, u32[]{:S(2)}) copy-start(bf16[4,2,2048,128]{3,2,1,0:T(8,128)(2,1)} %scatter_fusion.1) | copy-start | bytes 12582916
  113.4 10.6 %copy-start.12 = (f32[4,2,32,2048]{3,2,1,0:T(8,128)S(1)}, f32[4,2,32,2048]{3,2,1,0:T(8,128)}, u32[]{:S(2)}) copy-start(f32[4,2,32,2048]{3,2,1,0:T(8,128)} %get-tuple-element.70) | copy-start | bytes 6291460
  124.1 6.0 %copy-start.4 = (f32[4,2,32,2048]{3,2,1,0:T(8,128)S(1)}, f32[4,2,32,2048]{3,2,1,0:T(8,128)}, u32[]{:S(2)}) copy-start(f32[4,2,32,2048]{3,2,1,0:T(8,128)} %get-tuple-element.68) | copy-start | bytes 6291460
  133.6 7.2 %copy-start.10 = (f32[4,2,32,2048]{3,2,1,0:T(8,128)S(1)}, f32[4,2,32,2048]{3,2,1,0:T(8,128)}, u32[]{:S(2)}) copy-start(f32[4,2,32,2048]{3,2,1,0:T(8,128)} %get-tuple-element.56) | copy-start | bytes 6291460
  133.6 7.2 %copy-start.11 = (f32[4,2,32,2048]{3,2,1,0:T(8,128)S(1)}, f32[4,2,32,2048]{3,2,1,0:T(8,128)}, u32[]{:S(2)}) copy-start(f32[4,2,32,2048]{3,2,1,0:T(8,128)} %get-tuple-element.58) | copy-start | bytes 6291460
  133.6 7.2 %copy-start.13 = (f32[4,2,32,2048]{3,2,1,0:T(8,128)S(1)}, f32[4,2,32,2048]{3,2,1,0:T(8,128)}, u32[]{:S(2)}) copy-start(f32[4,2,32,2048]{3,2,1,0:T(8,128)} %get-tuple-element.70) | copy-start | bytes 6291460
  140.9 2.2 copy-start.5
  147.9 9.7 %all-to-all-start.1 = ((f32[1,8,64]{2,0,1:T(1,128)}), f32[1,8,64]{2,0,1:T(1,128)S(1)}, u32[]{:S(2)}, u32[]{:S(2)}) async-start(f32[1,8,64]{2,0,1:T(1,128)} %all_to_all.101), calls=%async_computation.1 | async-start | bytes 8192 | tf_op jit(solution)/shard_map/all_to_all | solution.py:66
  157.5 9.8 %all-to-all-start.4 = ((f32[1,8,64]{2,0,1:T(1,128)}), f32[1,8,64]{2,0,1:T(1,128)S(1)}, u32[]{:S(2)}, u32[]{:S(2)}) async-start(f32[1,8,64]{2,0,1:T(1,128)} %all_to_all.109), calls=%async_computation.4 | async-start | bytes 8192 | tf_op jit(solution)/shard_map/all_to_all | solution.py:66
  167.3 9.7 %all-to-all-start.5 = ((f32[1,8,64]{2,0,1:T(1,128)}), f32[1,8,64]{2,0,1:T(1,128)S(1)}, u32[]{:S(2)}, u32[]{:S(2)}) async-start(f32[1,8,64]{2,0,1:T(1,128)} %all_to_all.112), calls=%async_computation.5 | async-start | bytes 8192 | tf_op jit(solution)/shard_map/all_to_all | solution.py:67
  177.0 9.7 %all-to-all-start.8 = ((f32[1,8,64]{2,0,1:T(1,128)}), f32[1,8,64]{2,0,1:T(1,128)S(1)}, u32[]{:S(2)}, u32[]{:S(2)}) async-start(f32[1,8,64]{2,0,1:T(1,128)} %all_to_all.120), calls=%async_computation.8 | async-start | bytes 8192 | tf_op jit(solution)/shard_map/all_to_all | solution.py:67
  186.7 9.7 %all-to-all-start.7 = ((f32[1,8,64]{2,0,1:T(1,128)}), f32[1,8,64]{2,0,1:T(1,128)S(1)}, u32[]{:S(2)}, u32[]{:S(2)}) async-start(f32[1,8,64]{2,0,1:T(1,128)} %all_to_all.117), calls=%async_computation.7 | async-start | bytes 8192 | tf_op jit(solution)/shard_map/all_to_all | solution.py:66
  196.3 11.6 %all-to-all-start = ((f32[1,512,128]{2,0,1:T(1,128)}), f32[1,512,128]{2,0,1:T(1,128)S(1)}, u32[]{:S(2)}, u32[]{:S(2)}) async-start(f32[1,512,128]{2,0,1:T(1,128)} %bitcast.6), calls=%async_computation | async-start | bytes 524288 | tf_op jit(solution)/shard_map/all_to_all | solution.py:68
  207.9 38.8 %all-to-all-start.3 = ((f32[1,512,128]{2,0,1:T(1,128)}), f32[1,512,128]{2,0,1:T(1,128)S(1)}, u32[]{:S(2)}, u32[]{:S(2)}) async-start(f32[1,512,128]{2,0,1:T(1,128)} %bitcast.43), calls=%async_computation.3 | async-start | bytes 524288 | tf_op jit(solution)/shard_map/all_to_all | solution.py:68
  246.8 39.8 %all-to-all-start.6 = ((f32[1,512,128]{2,0,1:T(1,128)}), f32[1,512,128]{2,0,1:T(1,128)S(1)}, u32[]{:S(2)}, u32[]{:S(2)}) async-start(f32[1,512,128]{2,0,1:T(1,128)} %bitcast.80), calls=%async_computation.6 | async-start | bytes 524288 | tf_op jit(solution)/shard_map/all_to_all | solution.py:68
where the time goes:
time: 338 us; the launch traced here: 336 us
  blocking collectives  148 us (44%)
  matrix products  62.7 us (19%)
  local copies, waits for them, and re-layouts  45.9 us (14%)
  waiting for transfers between devices  36.6 us (11%)
  starting transfers between devices  35 us (10%)
  other arithmetic  7.3 us (2%)
    all_gather x3, blocking collectives, spread_merge(): gathered = lax.all_gather(merged, 'seq', axis=0, tiled=True)  94.5 us
    psum x1, blocking collectives, per_device(): lax.psum(partial_kv, 'seq').astype(jnp.bfloat16)  38.5 us
    dot_general x12, matrix products, attend(): jnp.einsum('bhqd,bhkd->bhqk', queries, keys, preferred_element_type=jnp.f...  31.3 us
    dot_general x12, matrix products, attend(): jnp.einsum('bhqk,bhkd->bhqd', weights, values, preferred_element_type=jnp...  21.6 us
    all_to_all x3, waiting for transfers between devices, spread_merge(): lax.all_to_all(maxima, 'seq', split_axis=1, concat_axis=0, tiled=True)  15.9 us
    scatter x3, local copies, waits for them, and re-layouts, per_device(): values_cache.at[batch_rows, :, targets, :]  15.8 us
    scatter x3, local copies, waits for them, and re-layouts, per_device(): keys_cache.at[batch_rows, :, targets, :]  15.6 us
    psum x1, blocking collectives, per_device(): summed = lax.psum(projected, 'tp')  14.8 us
  transfers between devices with their start and end apart: 9, of which 6 were waited for; matrix products, arithmetic and copies ran while one was open for 26% of the time, Pallas kernels for 0%

commit v1 on v0

v1 whole, which is shorter than its diff:
```python
import functools
import math

import jax
import jax.numpy as jnp
from jax import lax
from jax.experimental import pallas as pl
from jax.experimental.pallas import tpu as pltpu
from jax.sharding import PartitionSpec as P

NEG = -1e30
LANES = 128
F32 = jnp.float32
BF16 = jnp.bfloat16


def onehot(rows, cols, source):
    r = lax.broadcasted_iota(jnp.int32, (rows, cols), 0)
    c = lax.broadcasted_iota(jnp.int32, (rows, cols), 1)
    return (source(r) == c).astype(F32).astype(BF16)


def kernel(cfg, *refs):
    (len_s, acc_s, hid_v, sc_v, qd_v, qv_v, wkv_h, wout_h, k_h, v_h, kl_h, vl_h, out_ref,
     wkv, wout, kc, vc, kl, vl, lowk, lowv, scores,
     fr_send, fr_recv, o_send, o_recv, st_send, st_recv, ag, amat, rs_send, rs_recv, fin,
     in_sem, kv_sem, frs_sem, frr_sem, os_sem, or_sem, ss_sem, sr_sem,
     ags_sem, agf_sem, agr_sem, rss_sem, rsr_sem, fs_sem, ffr_sem) = refs
    n, tp, batch, heads, rounds, R, group, S, HD, split_cols = cfg
    pairs = batch * heads
    k = n // pairs
    rows1 = rounds * group * R
    rows = 2 * rows1
    fpad = fr_send.shape[1]
    pad_rows = st_send.shape[2]
    me = lax.axis_index("seq")
    tpi = lax.axis_index("tp")
    mine = lax.div(me, k)
    sub = lax.rem(me, k)
    MESH = pl.DeviceIdType.MESH

    cp_wkv = pltpu.make_async_copy(wkv_h, wkv, in_sem.at[0])
    cp_wkv.start()
    cp_wout = pltpu.make_async_copy(wout_h, wout, in_sem.at[1])

    def cache_copies(p):
        b = lax.div(p, heads)
        h = lax.rem(p, heads)
        return [
            pltpu.make_async_copy(src.at[b, h], dst.at[p], kv_sem.at[j, p])
            for j, (src, dst) in enumerate(((kl_h, kl), (k_h, kc), (vl_h, vl), (v_h, vc)))
        ]

    for step in range(1, pairs + 1):
        for c in cache_copies(lax.rem(mine + step, pairs)):
            c.start()
    cp_wout.start()

    barrier = pltpu.get_barrier_semaphore()
    for j in range(1, n):
        pl.semaphore_signal(barrier, inc=1, device_id={"seq": lax.rem(me + j, n)}, device_id_type=MESH)
    for j in range(1, tp):
        pl.semaphore_signal(barrier, inc=1, device_id={"tp": lax.rem(tpi + j, tp)}, device_id_type=MESH)

    tok = rounds * batch * R

    def fresh_source(r):
        b, q = r // fpad, r % fpad
        return jnp.where(q < rounds * R, (q // R) * (batch * R) + b * R + q % R, tok)

    hid = jnp.dot(onehot(batch * fpad, tok, fresh_source), hid_v[...], preferred_element_type=F32).astype(BF16)
    cp_wkv.wait()
    partial = jnp.dot(hid, wkv[...], preferred_element_type=F32)
    for p in range(pairs):
        b, h = p // heads, p % heads
        fr_send[p] = partial[b * fpad:(b + 1) * fpad, h * 2 * HD:(h + 1) * 2 * HD]
    pl.semaphore_wait(barrier, n - 1 + tp - 1)

    def fresh_copy(dst, slot):
        return pltpu.make_async_remote_copy(
            src_ref=fr_send.at[lax.div(dst, k)], dst_ref=fr_recv.at[slot],
            send_sem=frs_sem.at[dst], recv_sem=frr_sem.at[slot],
            device_id={"seq": dst}, device_id_type=MESH)

    for j in range(1, n):
        fresh_copy(lax.rem(me + j, n), me).start()
    fr_recv[me] = fr_send[mine]

    factor = (1.0 / math.sqrt(HD)) * math.log2(math.e)
    nch = S // LANES
    eye = (lax.broadcasted_iota(jnp.int32, (LANES, LANES), 0)
           == lax.broadcasted_iota(jnp.int32, (LANES, LANES), 1))
    spot = lax.broadcasted_iota(jnp.int32, (1, S), 1)

    def to_row(col):
        parts = []
        for c in range(pad_rows // LANES):
            lo, hi = c * LANES, min((c + 1) * LANES, rows)
            piece = jnp.where(eye[: hi - lo], col[lo:hi], 0.0)
            parts.append(jnp.sum(piece, axis=0, keepdims=True))
        return jnp.concatenate(parts, axis=1)

    def to_col(row):
        parts = []
        for c in range(pad_rows // LANES):
            lo, hi = c * LANES, min((c + 1) * LANES, rows)
            piece = jnp.where(eye[: hi - lo], row[:, lo:lo + LANES], 0.0)
            parts.append(jnp.sum(piece, axis=1, keepdims=True))
        return jnp.concatenate(parts, axis=0)

    def one_kind(q, keys, values, usable):
        s = lax.dot_general(q, keys, (((1,), (1,)), ((), ())), preferred_element_type=F32)
        s = jnp.where(usable, s * factor, NEG)
        m = jnp.max(s, axis=1, keepdims=True)
        w = jnp.where(usable, jnp.exp2(s - m), 0.0).astype(BF16)
        l = jnp.sum(w.astype(F32), axis=1, keepdims=True)
        o = jnp.dot(w, values, preferred_element_type=F32)
        return m, l, o

    def o_copy(p, dst, slot, src):
        return pltpu.make_async_remote_copy(
            src_ref=src, dst_ref=o_recv.at[slot], send_sem=os_sem.at[dst], recv_sem=or_sem.at[slot],
            device_id={"seq": dst}, device_id_type=MESH)

    def s_copy(p, dst, slot, src):
        return pltpu.make_async_remote_copy(
            src_ref=src, dst_ref=st_recv.at[slot], send_sem=ss_sem.at[dst], recv_sem=sr_sem.at[slot],
            device_id={"seq": dst}, device_id_type=MESH)

    def pair_part(p, o_dst, st_dst):
        b = lax.div(p, heads)
        h = lax.rem(p, heads)
        for c in cache_copies(p):
            c.wait()
        scales = sc_v[p].T
        for c in range(nch):
            sl = slice(c * LANES, (c + 1) * LANES)
            lowk[sl] = (kl[p, sl].astype(F32) * scales[:, c:c + 1]).astype(BF16)
            lowv[sl] = (vl[p, sl].astype(F32) * scales[:, nch + c:nch + c + 1]).astype(BF16)
        usable = (spot + me * S) < len_s[b]
        parts = [
            one_kind(qd_v[:, b, h].reshape(rows1, HD), lowk[...], lowv[...], usable),
            one_kind(qv_v[:, b, h].reshape(rows1, HD), kc[p], vc[p], usable),
        ]
        lses = []
        for j, (m, l, o) in enumerate(parts):
            some = l > 0.0
            safe = jnp.where(some, l, 1.0)
            o_dst[j * rows1:(j + 1) * rows1] = (o / safe).astype(BF16)
            lses.append(jnp.where(some, m + jnp.log2(safe), NEG))
        st_dst[...] = jnp.broadcast_to(to_row(jnp.concatenate(lses, axis=0)), st_dst.shape)

    @pl.loop(1, pairs)
    def _(step):
        p = lax.rem(mine + step, pairs)
        pair_part(p, o_send.at[p], st_send.at[p])
        for e in range(k):
            dst = p * k + lax.rem(sub + e, k)
            o_copy(p, dst, me, o_send.at[p]).start()
            s_copy(p, dst, me, st_send.at[p]).start()

    pair_part(mine, o_recv.at[me], st_recv.at[me])
    for e in range(1, k):
        dst = mine * k + lax.rem(sub + e, k)
        o_copy(mine, dst, me, o_recv.at[me]).start()
        s_copy(mine, dst, me, st_recv.at[me]).start()

    for j in range(1, n):
        fresh_copy(lax.rem(me + j, n), lax.rem(me + j, n)).wait_recv()
    total = fr_recv[0]
    for j in range(1, n):
        total = total + fr_recv[j]
    new_k = total[:, :HD].astype(BF16)
    new_v = total[:, HD:].astype(BF16)
    bm = lax.div(mine, heads)
    hm = lax.rem(mine, heads)
    r_id = lax.broadcasted_iota(jnp.int32, (rows1, fpad), 0)
    c_id = lax.broadcasted_iota(jnp.int32, (rows1, fpad), 1)
    turn, i_q = r_id // (group * R), r_id % R
    c_turn, c_j = c_id // R, c_id % R
    limit = jnp.zeros((rows1, fpad), jnp.int32)
    for t in range(rounds - 1):
        limit = jnp.where(c_turn == t, acc_s[t, bm], limit)
    see = ((c_turn < turn) & (c_j < limit)) | ((c_turn == turn) & (c_j <= i_q))
    dpart = one_kind(qd_v[:, bm, hm].reshape(rows1, HD), new_k, new_v, see)
    vpart = one_kind(qv_v[:, bm, hm].reshape(rows1, HD), new_k, new_v, see)
    M, L, O = (jnp.concatenate([a, b], axis=0) for a, b in zip(dpart, vpart))
    for j in range(n):
        src = lax.rem(me + j, n)
        if j:
            o_copy(mine, src, src, o_send.at[0]).wait_recv()
            s_copy(mine, src, src, st_send.at[0]).wait_recv()
        lse = to_col(st_recv[src][0:1])
        top = jnp.maximum(M, lse)
        wa = jnp.exp2(M - top)
        wb = jnp.where(lse > 0.5 * NEG, jnp.exp2(lse - top), 0.0)
        L = L * wa + wb
        O = O * wa + o_recv[src].astype(F32) * wb
        M = top
    ag[mine] = (O / L).astype(BF16)

    partner = mine + 1 - 2 * lax.rem(mine, 2)

    def ag_copy(slot, to, sem):
        return pltpu.make_async_remote_copy(
            src_ref=ag.at[slot], dst_ref=ag.at[slot], send_sem=sem, recv_sem=agr_sem.at[slot],
            device_id={"seq": to * k + sub}, device_id_type=MESH)

    others = [lax.rem(mine + 2 * j, pairs) for j in range(1, pairs // 2)]
    order = sorted(range(len(others)), key=lambda j: abs(j + 1 - pairs / 4))
    for j in order:
        ag_copy(mine, others[j], ags_sem.at[others[j]]).start()
    ag_copy(mine, partner, ags_sem.at[partner]).start()

    g24 = 2 * rounds * R

    def pair_source(r):
        g, q = r // g24, r % g24
        kind, q = q // (rounds * R), q % (rounds * R)
        return kind * rows1 + (q // R) * (group * R) + g * R + q % R

    perm = onehot(rows, rows, pair_source)

    def place(slot):
        b = lax.div(slot, heads)
        h = lax.rem(slot, heads)
        y = jnp.dot(perm, ag[slot], preferred_element_type=F32)
        at = pl.ds(pl.multiple_of(b * g24, g24), g24)
        for g in range(group):
            amat[h, at, g * HD:(g + 1) * HD] = y[g * g24:(g + 1) * g24]

    place(mine)
    far = [others[j] for j in reversed(range(len(others)))]
    for q in far:
        ag_copy(q, partner, agf_sem.at[q]).wait_recv()
        ag_copy(q, partner, agf_sem.at[q]).start()
        place(q)
    for q in [partner] + [lax.rem(partner + 2 * j, pairs) for j in range(1, pairs // 2)]:
        ag_copy(q, partner, agf_sem.at[q]).wait_recv()
        place(q)

    tokens = batch * g24

    def out_source(r):
        t, q = r // (2 * batch * R), r % (2 * batch * R)
        kind, q = q // (batch * R), q % (batch * R)
        return (q // R) * g24 + kind * (rounds * R) + t * R + q % R

    operm = onehot(tokens, tokens, out_source)
    lhs = [
        jnp.dot(operm, amat[h].astype(BF16), preferred_element_type=F32).astype(BF16)
        for h in range(heads)
    ]
    cp_wout.wait()
    depth = group * HD

    def project(cols):
        acc = jnp.dot(lhs[0], wout[0:depth, cols], preferred_element_type=F32)
        for h in range(1, heads):
            acc += jnp.dot(lhs[h], wout[h * depth:(h + 1) * depth, cols], preferred_element_type=F32)
        return acc

    def rs_copy(src, to, slot):
        return pltpu.make_async_remote_copy(
            src_ref=rs_send.at[src], dst_ref=rs_recv.at[slot], send_sem=rss_sem.at[to],
            recv_sem=rsr_sem.at[slot], device_id={"tp": to}, device_id_type=MESH)

    def fin_copy(to, slot):
        return pltpu.make_async_remote_copy(
            src_ref=fin.at[slot], dst_ref=fin.at[slot], send_sem=fs_sem.at[to],
            recv_sem=ffr_sem.at[slot], device_id={"tp": to}, device_id_type=MESH)

    peers = [lax.rem(tpi + j, tp) for j in range(1, tp)]
    if split_cols:
        width = rs_send.shape[2]
        chunk = lambda c: pl.ds(pl.multiple_of(c * width, LANES), width)
        for c in peers:
            rs_send[c] = project(chunk(c)).astype(BF16)
            rs_copy(c, c, tpi).start()
        own = project(chunk(tpi))
        for c in peers:
            rs_copy(c, c, c).wait_recv()
            own = own + rs_recv[c].astype(F32)
        fin[tpi] = own.astype(BF16)
        for c in peers:
            fin_copy(c, tpi).start()
        for c in peers:
            fin_copy(c, c).wait_recv()
        for c in range(tp):
            out_ref[:, c * width:(c + 1) * width] = fin[c]
        for c in peers:
            fin_copy(c, tpi).wait_send()
            rs_copy(c, c, tpi).wait_send()
    else:
        own = project(slice(None))
        rs_send[0] = own.astype(BF16)
        for c in peers:
            rs_copy(0, c, tpi).start()
        for c in peers:
            rs_copy(0, c, c).wait_recv()
        rs_recv[tpi] = rs_send[0]
        total = rs_recv[0].astype(F32)
        for c in range(1, tp):
            total = total + rs_recv[c].astype(F32)
        out_ref[...] = total.astype(BF16)
        for c in peers:
            rs_copy(0, c, tpi).wait_send()

    for j in range(1, n):
        dst = lax.rem(me + j, n)
        fresh_copy(dst, me).wait_send()
        o_copy(0, dst, me, o_send.at[0]).wait_send()
        s_copy(0, dst, me, st_send.at[0]).wait_send()
    for q in others:
        ag_copy(mine, q, ags_sem.at[q]).wait_send()
        ag_copy(q, partner, agf_sem.at[q]).wait_send()
    ag_copy(mine, partner, ags_sem.at[partner]).wait_send()


def per_device(n, tp, hidden_new, w_kv, w_out, queries_draft, queries_verify, keys_cache,
               values_cache, key_levels, value_levels, key_scales, value_scales, lengths, accepted):
    batch, heads, S, HD = keys_cache.shape
    rounds = hidden_new.shape[0]
    R = hidden_new.shape[1] // batch
    group = queries_draft.shape[3] // R
    pairs = batch * heads
    feats = hidden_new.shape[2]
    cols = w_out.shape[1]
    rows = 2 * rounds * group * R
    tokens = 2 * rounds * batch * R
    fpad = -(-rounds * R // 16) * 16
    pad_rows = -(-rows // LANES) * LANES
    split_cols = cols % (tp * LANES) == 0
    width = cols // tp if split_cols else cols
    cfg = (n, tp, batch, heads, rounds, R, group, S, HD, split_cols)
    scales = jnp.concatenate(
        [key_scales.reshape(pairs, S // LANES, LANES), value_scales.reshape(pairs, S // LANES, LANES)], axis=1)
    vm = pl.BlockSpec(memory_space=pltpu.VMEM)
    sm = pl.BlockSpec(memory_space=pltpu.SMEM)
    hb = pl.BlockSpec(memory_space=pl.ANY)
    dma = lambda *shape: pltpu.SemaphoreType.DMA(shape)
    out = pl.pallas_call(
        functools.partial(kernel, cfg),
        out_shape=jax.ShapeDtypeStruct((tokens, cols), BF16),
        in_specs=[sm, sm, vm, vm, vm, vm, hb, hb, hb, hb, hb, hb],
        out_specs=vm,
        scratch_shapes=[
            pltpu.VMEM((feats, heads * 2 * HD), BF16),
            pltpu.VMEM(w_out.shape, BF16),
            pltpu.VMEM((pairs, S, HD), BF16),
            pltpu.VMEM((pairs, S, HD), BF16),
            pltpu.VMEM((pairs, S, HD), BF16),
            pltpu.VMEM((pairs, S, HD), BF16),
            pltpu.VMEM((S, HD), BF16),
            pltpu.VMEM((S, HD), BF16),
            pltpu.VMEM((8, LANES), F32),
            pltpu.VMEM((pairs, fpad, 2 * HD), F32),
            pltpu.VMEM((n, fpad, 2 * HD), F32),
            pltpu.VMEM((pairs, rows, HD), BF16),
            pltpu.VMEM((n, rows, HD), BF16),
            pltpu.VMEM((pairs, 8, pad_rows), F32),
            pltpu.VMEM((n, 8, pad_rows), F32),
            pltpu.VMEM((pairs, rows, HD), BF16),
            pltpu.VMEM((heads, batch * 2 * rounds * R, group * HD), F32),
            pltpu.VMEM((tp, tokens, width), BF16),
            pltpu.VMEM((tp, tokens, width), BF16),
            pltpu.VMEM((tp, tokens, width), BF16),
            dma(2), dma(4, pairs), dma(n), dma(n), dma(n), dma(n), dma(n), dma(n),
            dma(pairs), dma(pairs), dma(pairs), dma(tp), dma(tp), dma(tp), dma(tp),
        ],
        compiler_params=pltpu.CompilerParams(
            collective_id=0, has_side_effects=True, vmem_limit_bytes=60 * 1024 * 1024),
    )(lengths, accepted, hidden_new.reshape(rounds * batch * R, feats), scales, queries_draft,
      queries_verify, w_kv.reshape(feats, heads * 2 * HD), w_out, keys_cache, values_cache,
      key_levels, value_levels)
    return out.reshape(rounds, 2, batch * R, cols)


def solution(mesh):
    return jax.shard_map(
        functools.partial(per_device, mesh.shape["seq"], mesh.shape["tp"]),
        mesh=mesh,
        in_specs=(
            P(None, None, "seq"),
            P("seq", "tp", None),
            P("tp", "seq"),
            P(None, None, "tp", None, None),
            P(None, None, "tp", None, None),
            P(None, "tp", "seq", None),
            P(None, "tp", "seq", None),
            P(None, "tp", "seq", None),
            P(None, "tp", "seq", None),
            P(None, "tp", "seq"),
            P(None, "tp", "seq"),
            P(),
            P(),
        ),
        out_specs=P(None, None, None, "seq"),
        check_vma=False,
    )
```

time: 338 us -> 58.1 us (0.17)
  blocking collectives: 148 us -> 0 us
  matrix products: 62.7 us -> 0 us
  Pallas kernels: 0 us -> 51.2 us
  local copies, waits for them, and re-layouts: 45.9 us -> 5.84 us
  waiting for transfers between devices: 36.6 us -> 0 us
  starting transfers between devices: 35 us -> 0 us
  other arithmetic: 7.3 us -> 0.67 us
    all_gather x3 -> x0, blocking collectives: 94.5 us -> none  [spread_merge(): gathered = lax.all_gather(merged, 'seq', axis=0, tiled=True)]
    dot_general x30 -> x0, matrix products: 62.7 us -> none  [the longest x12 31.3 us: attend(): jnp.einsum('bhqd,bhkd->bhqk', queries, keys, preferred_element_type=jnp.f...]
    psum x2 -> x0, blocking collectives: 53.4 us -> none  [the longest x1 38.5 us: per_device(): lax.psum(partial_kv, 'seq').astype(jnp.bfloat16)]
    pallas_call x0 -> x1, Pallas kernels: none -> 51.2 us  [per_device(): pl.pallas_call(functools.partial(kernel, cfg), out_shape=jax.ShapeDtypeSt...]
    all_to_all x9 -> x0, waiting for transfers between devices: 36.6 us -> none  [the longest x3 15.9 us: spread_merge(): lax.all_to_all(maxima, 'seq', split_axis=1, concat_axis=0, tiled=True)]
    all_to_all x9 -> x0, starting transfers between devices: 35 us -> none  [the longest x3 13.9 us: spread_merge(): lax.all_to_all(totals, 'seq', split_axis=1, concat_axis=0, tiled=True)]
    scatter x6 -> x0, local copies, waits for them, and re-layouts: 31.4 us -> none  [the longest x3 15.8 us: per_device(): values_cache.at[batch_rows, :, targets, :]]
    unnamed x53 -> x2, local copies, waits for them, and re-layouts: 9.41 us -> 4.06 us
  transfers between devices with their start and end apart: 9 -> 0, of which waited for: 6 -> 0; matrix products, arithmetic and copies ran while one was open for 26% -> 0% of each run, Pallas kernels for 0% -> 0%
where the time goes in v1:
time: 58.1 us; the launch traced here: 57.8 us
  Pallas kernels  51.2 us (88%)
  local copies, waits for them, and re-layouts  5.84 us (10%)
  other arithmetic  0.67 us (1%)
    pallas_call x1, Pallas kernels, per_device(): pl.pallas_call(functools.partial(kernel, cfg), out_shape=jax.ShapeDtypeSt...  51.2 us
    unnamed x2, local copies, waits for them, and re-layouts  4.06 us

profile of v1, /device:TPU:0, one launch (start us, length us, event | category | flops | bytes accessed | tf_op | source)
XLA Modules:
  0.0 57.8 jit_solution(5593376525887052446)
XLA Ops:
  0.0 0.9 %reshape.16 = f32[8,16,128]{2,1,0:T(8,128)S(1)} reshape(f32[4,2,2048]{2,1,0:T(2,128)} %param.22) | data formatting | bytes 131072 | tf_op jit(solution)/shard_map/reshape | solution.py:337
  0.9 0.9 %reshape.17 = f32[8,16,128]{2,1,0:T(8,128)S(1)} reshape(f32[4,2,2048]{2,1,0:T(2,128)} %param.23) | data formatting | bytes 131072 | tf_op jit(solution)/shard_map/reshape | solution.py:337
  1.8 0.7 %pad_maximum_fusion.refs_3_ = f32[8,32,128]{2,1,0:T(8,128)} fusion(f32[8,16,128]{2,1,0:T(8,128)S(1)} %reshape.17, f32[8,16,128]{2,1,0:T(8,128)S(1)} %reshape.16), kind=kLoop, calls=%fused_computation | loop fusion | flops 32768 | bytes 262144 | tf_op jit(solution)/shard_map/concatenate | solution.py:336
  2.5 2.4 %copy.14 = bf16[128,8,2,256]{3,1,2,0:T(8,128)(2,1)} copy(bf16[128,8,2,256]{3,2,1,0:T(2,128)(2,1)} %bitcast.5) | data formatting | bytes 2097152
  4.9 51.2 %shard_map.127 = bf16[96,1024]{1,0:T(8,128)(2,1)} custom-call(s32[4]{0:T(128)} %refs_0_.1, s32[2,4]{1,0:T(2,128)} %refs_1_.1, bf16[48,1024]{1,0:T(8,128)(2,1)} %bitcast.7, f32[8,32,128]{2,1,0:T(8,128)} %pad_maximum_fusion.refs_3_, bf16[3,4,2,32,128]{4,3,2,1,0:T(8,128)(2,1)} %refs_4_.1, bf16[3,4,2,32,128]{4,3,2,1,0:T(8,128)(2,1)} %refs_5_.1, ...), custom_call_target="tpu_custom_call" | custom-call | tf_op jit(solution)/shard_map/pallas_call | solution.py:342
  56.1 1.6 %copy.16 = bf16[3,2,16,1024]{3,2,1,0:T(8,128)(2,1)} copy(bf16[3,2,16,1024]{3,2,1,0:T(8,128)(2,1)} %bitcast.6) | data formatting | bytes 393216

commit v2 on v1

--- a/solution.py
+++ b/solution.py
@@ -21,7 +21,7 @@
 
 
 def kernel(cfg, *refs):
-    (len_s, acc_s, hid_v, sc_v, qd_v, qv_v, wkv_h, wout_h, k_h, v_h, kl_h, vl_h, out_ref,
+    (len_s, acc_s, hid_v, ks_v, vs_v, qd_v, qv_v, wkv_h, wout_h, k_h, v_h, kl_h, vl_h, out_ref,
      wkv, wout, kc, vc, kl, vl, lowk, lowv, scores,
      fr_send, fr_recv, o_send, o_recv, st_send, st_recv, ag, amat, rs_send, rs_recv, fin,
      in_sem, kv_sem, frs_sem, frr_sem, os_sem, or_sem, ss_sem, sr_sem,
@@ -70,7 +70,8 @@
 
     hid = jnp.dot(onehot(batch * fpad, tok, fresh_source), hid_v[...], preferred_element_type=F32).astype(BF16)
     cp_wkv.wait()
-    partial = jnp.dot(hid, wkv[...], preferred_element_type=F32)
+    partial = jnp.concatenate(
+        [jnp.dot(hid, wkv[:, h, :], preferred_element_type=F32) for h in range(heads)], axis=1)
     for p in range(pairs):
         b, h = p // heads, p % heads
         fr_send[p] = partial[b * fpad:(b + 1) * fpad, h * 2 * HD:(h + 1) * 2 * HD]
@@ -87,10 +88,8 @@
     fr_recv[me] = fr_send[mine]
 
     factor = (1.0 / math.sqrt(HD)) * math.log2(math.e)
-    nch = S // LANES
     eye = (lax.broadcasted_iota(jnp.int32, (LANES, LANES), 0)
            == lax.broadcasted_iota(jnp.int32, (LANES, LANES), 1))
-    spot = lax.broadcasted_iota(jnp.int32, (1, S), 1)
 
     def to_row(col):
         parts = []
@@ -110,12 +109,11 @@
 
     def one_kind(q, keys, values, usable):
         s = lax.dot_general(q, keys, (((1,), (1,)), ((), ())), preferred_element_type=F32)
-        s = jnp.where(usable, s * factor, NEG)
-        m = jnp.max(s, axis=1, keepdims=True)
-        w = jnp.where(usable, jnp.exp2(s - m), 0.0).astype(BF16)
-        l = jnp.sum(w.astype(F32), axis=1, keepdims=True)
-        o = jnp.dot(w, values, preferred_element_type=F32)
-        return m, l, o
+        s = jnp.where(usable, s, NEG)
+        m = jnp.max(s, axis=1, keepdims=True) * factor
+        w = jnp.exp2(s * factor - m).astype(BF16)
+        both = jnp.dot(w, jnp.concatenate([values, jnp.ones(values.shape, BF16)], axis=1), preferred_element_type=F32)
+        return m, both[:, HD:HD + 1], both[:, :HD]
 
     def o_copy(p, dst, slot, src):
         return pltpu.make_async_remote_copy(
@@ -132,23 +130,31 @@
         h = lax.rem(p, heads)
         for c in cache_copies(p):
             c.wait()
-        scales = sc_v[p].T
-        for c in range(nch):
-            sl = slice(c * LANES, (c + 1) * LANES)
-            lowk[sl] = (kl[p, sl].astype(F32) * scales[:, c:c + 1]).astype(BF16)
-            lowv[sl] = (vl[p, sl].astype(F32) * scales[:, nch + c:nch + c + 1]).astype(BF16)
-        usable = (spot + me * S) < len_s[b]
-        parts = [
-            one_kind(qd_v[:, b, h].reshape(rows1, HD), lowk[...], lowv[...], usable),
-            one_kind(qv_v[:, b, h].reshape(rows1, HD), kc[p], vc[p], usable),
-        ]
-        lses = []
-        for j, (m, l, o) in enumerate(parts):
-            some = l > 0.0
-            safe = jnp.where(some, l, 1.0)
-            o_dst[j * rows1:(j + 1) * rows1] = (o / safe).astype(BF16)
-            lses.append(jnp.where(some, m + jnp.log2(safe), NEG))
-        st_dst[...] = jnp.broadcast_to(to_row(jnp.concatenate(lses, axis=0)), st_dst.shape)
+        count = len_s[b] - me * S
+
+        def some(span):
+            chunks = span // LANES
+            kr, vr = (jnp.where(h == 0, r[b, 0:1, :span], r[b, heads - 1:heads, :span]) for r in (ks_v, vs_v))
+            cut = [x[:, c * LANES:(c + 1) * LANES] for x in (kr, vr) for c in range(chunks)]
+            cut += [cut[0]] * (-len(cut) % 8)
+            scales = jnp.concatenate(cut, axis=0).T
+            for c in range(chunks):
+                sl = slice(c * LANES, (c + 1) * LANES)
+                lowk[sl] = (kl[p, sl].astype(F32) * scales[:, c:c + 1]).astype(BF16)
+                lowv[sl] = (vl[p, sl].astype(F32) * scales[:, chunks + c:chunks + c + 1]).astype(BF16)
+            usable = lax.broadcasted_iota(jnp.int32, (1, span), 1) < count
+            al = slice(0, span)
+            parts = [
+                one_kind(qd_v[:, b, h].reshape(rows1, HD), lowk[al], lowv[al], usable),
+                one_kind(qv_v[:, b, h].reshape(rows1, HD), kc[p, al], vc[p, al], usable),
+            ]
+            lses = []
+            for j, (m, l, o) in enumerate(parts):
+                o_dst[j * rows1:(j + 1) * rows1] = (o / l).astype(BF16)
+                lses.append(jnp.where(jnp.full(m.shape, count) > 0, m + jnp.log2(l), NEG))
+            st_dst[...] = jnp.broadcast_to(to_row(jnp.concatenate(lses, axis=0)), st_dst.shape)
+
+        some(S)
 
     @pl.loop(1, pairs)
     def _(step):
@@ -229,11 +235,12 @@
         for g in range(group):
             amat[h, at, g * HD:(g + 1) * HD] = y[g * g24:(g + 1) * g24]
 
-    place(mine)
     far = [others[j] for j in reversed(range(len(others)))]
     for q in far:
         ag_copy(q, partner, agf_sem.at[q]).wait_recv()
         ag_copy(q, partner, agf_sem.at[q]).start()
+    place(mine)
+    for q in far:
         place(q)
     for q in [partner] + [lax.rem(partner + 2 * j, pairs) for j in range(1, pairs // 2)]:
         ag_copy(q, partner, agf_sem.at[q]).wait_recv()
@@ -333,8 +340,6 @@
     split_cols = cols % (tp * LANES) == 0
     width = cols // tp if split_cols else cols
     cfg = (n, tp, batch, heads, rounds, R, group, S, HD, split_cols)
-    scales = jnp.concatenate(
-        [key_scales.reshape(pairs, S // LANES, LANES), value_scales.reshape(pairs, S // LANES, LANES)], axis=1)
     vm = pl.BlockSpec(memory_space=pltpu.VMEM)
     sm = pl.BlockSpec(memory_space=pltpu.SMEM)
     hb = pl.BlockSpec(memory_space=pl.ANY)
@@ -342,10 +347,10 @@
     out = pl.pallas_call(
         functools.partial(kernel, cfg),
         out_shape=jax.ShapeDtypeStruct((tokens, cols), BF16),
-        in_specs=[sm, sm, vm, vm, vm, vm, hb, hb, hb, hb, hb, hb],
+        in_specs=[sm, sm, vm, vm, vm, vm, vm, hb, hb, hb, hb, hb, hb],
         out_specs=vm,
         scratch_shapes=[
-            pltpu.VMEM((feats, heads * 2 * HD), BF16),
+            pltpu.VMEM(w_kv.shape, BF16),
             pltpu.VMEM(w_out.shape, BF16),
             pltpu.VMEM((pairs, S, HD), BF16),
             pltpu.VMEM((pairs, S, HD), BF16),
@@ -370,8 +375,8 @@
         ],
         compiler_params=pltpu.CompilerParams(
             collective_id=0, has_side_effects=True, vmem_limit_bytes=60 * 1024 * 1024),
-    )(lengths, accepted, hidden_new.reshape(rounds * batch * R, feats), scales, queries_draft,
-      queries_verify, w_kv.reshape(feats, heads * 2 * HD), w_out, keys_cache, values_cache,
+    )(lengths, accepted, hidden_new.reshape(rounds * batch * R, feats), key_scales, value_scales, queries_draft,
+      queries_verify, w_kv, w_out, keys_cache, values_cache,
       key_levels, value_levels)
     return out.reshape(rounds, 2, batch * R, cols)
 

time: 58.1 us -> 51.6 us (0.89)
  local copies, waits for them, and re-layouts: 5.84 us -> 1.62 us
  Pallas kernels: 51.2 us -> 49.4 us
  other arithmetic: 0.67 us -> 0 us
    unnamed x2 -> x1, local copies, waits for them, and re-layouts: 4.06 us -> 1.62 us
    pallas_call x1, Pallas kernels: 51.2 us -> 49.4 us  [per_device(): pl.pallas_call(functools.partial(kernel, cfg), out_shape=jax.ShapeDtypeSt...]
    reshape x2 -> x0, local copies, waits for them, and re-layouts: 1.79 us -> none  [the longest x1 0.89 us: per_device(): value_scales.reshape(pairs, S // LANES, LANES)]
    concatenate x1 -> x0, other arithmetic: 0.67 us -> none  [per_device(): jnp.concatenate([key_scales.reshape(pairs, S // LANES, LANES), value_scal...]
where the time goes in v2:
time: 51.6 us; the launch traced here: 51 us
  Pallas kernels  49.4 us (96%)
  local copies, waits for them, and re-layouts  1.62 us (3%)
    pallas_call x1, Pallas kernels, per_device(): pl.pallas_call(functools.partial(kernel, cfg), out_shape=jax.ShapeDtypeSt...  49.4 us
    unnamed x1, local copies, waits for them, and re-layouts  1.62 us

profile of v2, /device:TPU:0, one launch (start us, length us, event | category | flops | bytes accessed | tf_op | source)
XLA Modules:
  0.0 51.0 jit_solution(3466504311843855609)
XLA Ops:
  0.0 49.4 %shard_map.127 = bf16[96,1024]{1,0:T(8,128)(2,1)} custom-call(s32[4]{0:T(128)} %refs_0_.1, s32[2,4]{1,0:T(2,128)} %refs_1_.1, bf16[48,1024]{1,0:T(8,128)(2,1)} %bitcast.3, f32[4,2,2048]{2,1,0:T(2,128)} %refs_3_.1, f32[4,2,2048]{2,1,0:T(2,128)} %refs_4_.1, bf16[3,4,2,32,128]{4,3,2,1,0:T(8,128)(2,1)} %refs_5_.1, bf16[3,4,2,32,128]{4,3,2,1,0:T(8,128)(2,1)} %refs_6_.1, ...), custom_call_target="tpu_custom_call" | custom-call | tf_op jit(solution)/shard_map/pallas_call | solution.py:347
  49.4 1.6 %copy.15 = bf16[3,2,16,1024]{3,2,1,0:T(8,128)(2,1)} copy(bf16[3,2,16,1024]{3,2,1,0:T(8,128)(2,1)} %bitcast.2) | data formatting | bytes 393216
